TPU v7x, 32 devices: a whole 2x2x4 slice. The times are simulated.
32 devices in a mesh: tp: 4 (over y, core), ad: 8 (over z, x).
Axes of the slice: x: 2, y: 2, z: 4, core: 2. Of those that a mesh axis runs over, the one named last changes fastest.
Arguments:
- hidden: bfloat16 [2048, 8192], P('ad'), may hold values from -6 to 6
- key_value_weight: bfloat16 [8192, 2048], P(None, 'tp'), may hold values from -0.0625 to 0.0625
- request_group: int32 [2048, 1], P('ad'), may hold values from 0 to 7; in each aligned block of 256 rows (0 to 255, 256 to 511, ...) at most 64 rows name the same one
- request_member: int32 [2048], P('ad'), may hold values from 0 to 3
- adapter_down_weight: bfloat16 [8192, 2048], P('tp', 'ad'), may hold values from -0.0625 to 0.0625
- adapter_up_weight: bfloat16 [2048, 2048], P('ad', 'tp'), may hold values from -0.75 to 0.75
Outputs:
- kv_out: bfloat16 [2048, 2048], P('ad', 'tp')
Inputs may be any that keep to these rules, and one draw needn't show every extreme that they name: `request_group`: among the 256 rows of one index of ad, no group is named by more than 64 rows, a bound that some block reaches.
All inputs are finite; a program needn't handle non-finite values.
Results may differ from a plain program's by a relative error of at most 0.007.
Values may be sent and summed in bfloat16 or wider, within the bound.
No kernel may reach another device: no remote copies, remote signals or barrier semaphores. Data moves between devices by JAX's collectives and lax.ppermute only.
A program may use at most 128 MiB of HBM per device.

v0:
```python
import jax
import jax.numpy as jnp
from jax import lax
from jax.sharding import PartitionSpec as P

ADAPTER_RANK = 64


def shards(
    hidden, key_value_weight, request_group, request_member, adapter_down_weight, adapter_up_weight
):
    column_portion = adapter_down_weight.shape[0]
    adapter_pool_count = adapter_down_weight.shape[1] // ADAPTER_RANK
    base_output = jnp.dot(hidden, key_value_weight, preferred_element_type=jnp.float32)
    own_cols = lax.dynamic_slice_in_dim(
        hidden, lax.axis_index("tp") * column_portion, column_portion, 1
    )
    owner_index = request_group[:, 0]
    adapter = owner_index * adapter_pool_count + request_member
    block_portion = lax.all_gather(adapter_down_weight, "ad", axis=1, tiled=True)
    column_total = block_portion.shape[1]
    scores = jnp.dot(own_cols, block_portion, preferred_element_type=jnp.float32)
    column = jnp.arange(column_total, dtype=jnp.int32)
    kept_mask = (column // ADAPTER_RANK)[None, :] == adapter[:, None]
    selector = (
        (column % ADAPTER_RANK)[:, None] == jnp.arange(ADAPTER_RANK, dtype=jnp.int32)[None, :]
    ).astype(jnp.float32)
    partial_ranks = jnp.dot(
        jnp.where(kept_mask, scores, 0.0), selector, precision=lax.Precision.HIGHEST
    )
    rank_values = lax.psum(partial_ranks, "tp").astype(jnp.bfloat16)
    block_portion = lax.all_gather(adapter_up_weight, "ad", axis=0, tiled=True)
    line_total = block_portion.shape[0]
    row_index = jnp.arange(line_total, dtype=jnp.int32)
    spread = (
        (row_index % ADAPTER_RANK)[None, :] == jnp.arange(ADAPTER_RANK, dtype=jnp.int32)[:, None]
    ).astype(jnp.bfloat16)
    widened = jnp.dot(rank_values, spread, preferred_element_type=jnp.float32)
    kept_mask = (row_index // ADAPTER_RANK)[None, :] == adapter[:, None]
    raised_output = jnp.where(kept_mask, widened, 0.0).astype(jnp.bfloat16)
    adapter_update = jnp.dot(
        raised_output, block_portion, preferred_element_type=jnp.float32
    ).astype(jnp.bfloat16)
    return (base_output + adapter_update.astype(jnp.float32)).astype(jnp.bfloat16)


def solution(mesh):
    placed = (P("ad", None), P(None, "tp"), P("ad", None), P("ad"), P("tp", "ad"), P("ad", "tp"))
    return jax.shard_map(
        shards, mesh=mesh, in_specs=placed, out_specs=P("ad", "tp"), check_vma=False
    )
```

profile of v0, /device:TPU:0, one launch (start us, length us, event | category | flops | bytes accessed | tf_op | source)
XLA Modules:
  0.0 203.6 jit_solution(13971514790394120517)
XLA Ops:
  6.5 0.0 all-gather.3.cloned.1.call-start
  6.5 0.7 all-gather.3.cloned.1.call-update
  7.3 0.0 all-gather.5.cloned.1.call-start
  7.3 0.7 all-gather.5.cloned.1.call-update
  8.0 0.7 broadcast_multiply_fusion
  8.7 0.7 add.34
  9.4 127.7 %all-gather.3.cloned.1.call-done = bf16[2048,2048]{1,0:T(8,128)(2,1)} async-done(((bf16[2048,256]{1,0:T(8,128)(2,1)}), bf16[2048,2048]{1,0:T(8,128)(2,1)}) %all-gather.3.cloned.1.call-update) | async-done | bytes 8388624 | tf_op jit(solution)/shard_map/all_gather | solution.py:20
  137.1 6.1 %compare_select_fusion = f32[256,2048]{1,0:T(8,128)S(1)} fusion(bf16[2048,2048]{1,0:T(8,128)(2,1)} %all-gather.3.cloned.1.call-done, bf16[256,8192]{1,0:T(8,128)(2,1)} %param.6, s32[]{:T(128)S(6)} %select_n.40, s32[2048]{0:T(1024)S(1)} %get-tuple-element.6, s32[256]{0:T(256)S(1)} %add.34), kind=kOutput, calls=%fused_computation.1 | convolution fusion | flops 2148532224 | bytes 11543556 | tf_op jit(solution)/shard_map/dot_general | solution.py:22
  143.1 1.2 fusion.9
  144.4 12.5 %psum.7 = bf16[256,64]{1,0:T(8,128)(2,1)S(1)} all-reduce(f32[256,64]{1,0:T(8,128)S(1)} %fusion.9), channel_id=1, replica_groups=mesh['tp'=4,'ad'=8] {'tp'}, use_global_device_ids=true, to_apply=%region_0.1 | all-reduce | flops 16384 | bytes 98304 | tf_op jit(solution)/shard_map/psum | solution.py:31
  156.9 29.6 %all-gather.5.cloned.1.call-done = bf16[2048,512]{1,0:T(8,128)(2,1)} async-done(((bf16[256,512]{1,0:T(8,128)(2,1)}), bf16[2048,512]{1,0:T(8,128)(2,1)}) %all-gather.5.cloned.1.call-update) | async-done | bytes 2097168 | tf_op jit(solution)/shard_map/all_gather | solution.py:32
  186.5 2.6 %fusion.4 = f32[256,512]{1,0:T(8,128)S(1)} fusion(bf16[2048,512]{1,0:T(8,128)(2,1)} %all-gather.5.cloned.1.call-done, s32[2048]{0:T(1024)S(1)} %get-tuple-element.6, s32[256]{0:T(256)S(1)} %add.34, s32[2048]{0:T(1024)S(1)} %get-tuple-element.5, bf16[256,64]{1,0:T(8,128)(2,1)S(1)} %psum.7), kind=kOutput, calls=%fused_computation.7 | convolution fusion | flops 605945856 | bytes 2671616 | tf_op jit(solution)/shard_map/dot_general | solution.py:41
  189.1 7.7 %fusion.2 = bf16[256,512]{1,0:T(8,128)(2,1)} fusion(f32[256,512]{1,0:T(8,128)S(1)} %fusion.4, bf16[256,8192]{1,0:T(8,128)(2,1)} %param.6, bf16[8192,512]{1,0:T(8,128)(2,1)} %param.7), kind=kOutput, calls=%fused_computation.5 | convolution fusion | flops 2147745792 | bytes 13369344 | tf_op jit(solution)/shard_map/dot_general | solution.py:14
  (1 shorter events, 0.0 us)
Async XLA Ops:
  6.5 130.5 %all-gather.3.cloned.1.call-start = ((), (), s32[]{:S(2)}) async-start(), calls=%async_computation | async-start | bytes 9437184 | tf_op jit(solution)/shard_map/all_gather | solution.py:20
  7.3 179.2 %all-gather.5.cloned.1.call-start = ((), (), s32[]{:S(2)}) async-start(), calls=%async_computation.1 | async-start | bytes 2359296 | tf_op jit(solution)/shard_map/all_gather | solution.py:32
Sparse Core Ops, SparseCore 0:
  9.4 127.6 all-gather.2
  139.2 47.2 all-gather.4
where the time goes:
time: 204 us
  waiting for transfers between devices  159 us (78%)
  matrix products  17.5 us (9%)
  between operations  13.4 us (7%)
  blocking collectives  12.5 us (6%)
    all_gather x1, waiting for transfers between devices, shards(): lax.all_gather(adapter_down_weight, 'ad', axis=1, tiled=True)  128 us
    all_gather x1, waiting for transfers between devices, shards(): block_portion = lax.all_gather(adapter_up_weight, 'ad', axis=0, tiled=True)  29.6 us
    psum x1, blocking collectives, shards(): rank_values = lax.psum(partial_ranks, 'tp').astype(jnp.bfloat16)  12.5 us
    dot_general x1, matrix products, shards(): jnp.dot(hidden, key_value_weight, preferred_element_type=jnp.float32)  7.69 us
    dot_general x1, matrix products, shards(): jnp.dot(own_cols, block_portion, preferred_element_type=jnp.float32)  6.06 us
  transfers between devices with their start and end apart: 2, of which 2 were waited for; matrix products, arithmetic and copies ran while one was open for 4% of the time, Pallas kernels for 0%

commit v1 on v0

--- a/solution.py
+++ b/solution.py
@@ -9,6 +9,19 @@
 def shards(
     hidden, key_value_weight, request_group, request_member, adapter_down_weight, adapter_up_weight
 ):
+
+    def end_the_sources_all(unit, link_axis):
+        n_blocks = lax.axis_size(link_axis)
+        r1 = sorted(((jj, (jj + 1) % n_blocks) for jj in range(n_blocks)))
+        formed = unit
+        cards = [formed]
+        for c in range(1, n_blocks):
+            formed = lax.ppermute(formed, link_axis, r1)
+            cards.insert(0, formed)
+        block_now = jnp.concatenate(cards, axis=1)
+        current_block = jnp.roll(block_now, (lax.axis_index(link_axis) + 1) * unit.shape[1], axis=1)
+        return current_block
+
     column_portion = adapter_down_weight.shape[0]
     adapter_pool_count = adapter_down_weight.shape[1] // ADAPTER_RANK
     base_output = jnp.dot(hidden, key_value_weight, preferred_element_type=jnp.float32)
@@ -17,7 +30,7 @@
     )
     owner_index = request_group[:, 0]
     adapter = owner_index * adapter_pool_count + request_member
-    block_portion = lax.all_gather(adapter_down_weight, "ad", axis=1, tiled=True)
+    block_portion = end_the_sources_all(adapter_down_weight, "ad")
     column_total = block_portion.shape[1]
     scores = jnp.dot(own_cols, block_portion, preferred_element_type=jnp.float32)
     column = jnp.arange(column_total, dtype=jnp.int32)

time: 204 us -> 244 us (1.20)
  waiting for transfers between devices: 159 us -> 183 us
  local copies, waits for them, and re-layouts: 0 us -> 15.2 us
  starting transfers between devices: 0.04 us -> 2.98 us
    ppermute x0 -> x7, waiting for transfers between devices: none -> 183 us  [end_the_sources_all(): formed = lax.ppermute(formed, link_axis, r1)]
    all_gather x1 -> x0, waiting for transfers between devices: 128 us -> none  [shards(): lax.all_gather(adapter_down_weight, 'ad', axis=1, tiled=True)]
    all_gather x1, waiting for transfers between devices: 29.6 us -> 0.02 us  [shards(): block_portion = lax.all_gather(adapter_up_weight, 'ad', axis=0, tiled=True)]
    unnamed x0 -> x29, local copies, waits for them, and re-layouts: none -> 15.1 us
    ppermute x0 -> x7, starting transfers between devices: none -> 2.98 us  [end_the_sources_all(): formed = lax.ppermute(formed, link_axis, r1)]
  transfers between devices with their start and end apart: 2 -> 8, of which waited for: 2 -> 7; matrix products, arithmetic and copies ran while one was open for 4% -> 8% of each run, Pallas kernels for 0% -> 0%
where the time goes in v1:
time: 244 us
  waiting for transfers between devices  183 us (75%)
  local copies, waits for them, and re-layouts  15.2 us (6%)
  matrix products  15.1 us (6%)
  between operations  13.6 us (6%)
  blocking collectives  12.2 us (5%)
  starting transfers between devices  2.98 us (1%)
    ppermute x7, waiting for transfers between devices, end_the_sources_all(): formed = lax.ppermute(formed, link_axis, r1)  183 us
    unnamed x29, local copies, waits for them, and re-layouts  15.1 us
    psum x1, blocking collectives, shards(): rank_values = lax.psum(partial_ranks, 'tp').astype(jnp.bfloat16)  12.2 us
    dot_general x1, matrix products, shards(): jnp.dot(hidden, key_value_weight, preferred_element_type=jnp.float32)  7.69 us
  transfers between devices with their start and end apart: 8, of which 7 were waited for; matrix products, arithmetic and copies ran while one was open for 8% of the time, Pallas kernels for 0%

profile of v1, /device:TPU:0, one launch (start us, length us, event | category | flops | bytes accessed | tf_op | source)
XLA Modules:
  0.0 243.7 jit_solution(13255932322002448835)
XLA Ops:
  6.5 0.0 all-gather.2.cloned.1.call-start
  6.5 3.0 %collective-permute-start = (bf16[2048,256]{1,0:T(8,128)(2,1)}, bf16[2048,256]{1,0:T(8,128)(2,1)S(1)}, u32[]{:S(2)}, u32[]{:S(2)}) collective-permute-start(bf16[2048,256]{1,0:T(8,128)(2,1)} %param.10), channel_id=1, source_target_pairs={{0,1},{1,2},{2,3},{3,4},{4,5},{5,6},{6,7},{7,0},{8,9},{9,10},{10,1... | collective-permute-start | bytes 3145736 | tf_op jit(solution)/shard_map/ppermute | solution.py:19
  9.5 26.5 %collective-permute-done = bf16[2048,256]{1,0:T(8,128)(2,1)S(1)} collective-permute-done((bf16[2048,256]{1,0:T(8,128)(2,1)}, bf16[2048,256]{1,0:T(8,128)(2,1)S(1)}, u32[]{:S(2)}, u32[]{:S(2)}) %collective-permute-start) | collective-permute-done | bytes 1048608 | tf_op jit(solution)/shard_map/ppermute | solution.py:19
  36.0 0.0 collective-permute-start.1
  36.0 27.0 %collective-permute-done.1 = bf16[2048,256]{1,0:T(8,128)(2,1)S(1)} collective-permute-done((bf16[2048,256]{1,0:T(8,128)(2,1)S(1)}, bf16[2048,256]{1,0:T(8,128)(2,1)S(1)}, u32[]{:S(2)}, u32[]{:S(2)}) %collective-permute-start.1) | collective-permute-done | bytes 1048608 | tf_op jit(solution)/shard_map/ppermute | solution.py:19
  63.0 0.0 collective-permute-start.2
  63.0 26.2 %collective-permute-done.2 = bf16[2048,256]{1,0:T(8,128)(2,1)S(1)} collective-permute-done((bf16[2048,256]{1,0:T(8,128)(2,1)S(1)}, bf16[2048,256]{1,0:T(8,128)(2,1)S(1)}, u32[]{:S(2)}, u32[]{:S(2)}) %collective-permute-start.2) | collective-permute-done | bytes 1048608 | tf_op jit(solution)/shard_map/ppermute | solution.py:19
  89.2 1.0 copy-done.1
  90.1 0.0 collective-permute-start.3
  90.1 25.3 %collective-permute-done.3 = bf16[2048,256]{1,0:T(8,128)(2,1)S(1)} collective-permute-done((bf16[2048,256]{1,0:T(8,128)(2,1)S(1)}, bf16[2048,256]{1,0:T(8,128)(2,1)S(1)}, u32[]{:S(2)}, u32[]{:S(2)}) %collective-permute-start.3) | collective-permute-done | bytes 1048608 | tf_op jit(solution)/shard_map/ppermute | solution.py:19
  115.4 1.0 copy-done.3
  116.4 0.0 collective-permute-start.4
  116.4 24.4 %collective-permute-done.4 = bf16[2048,256]{1,0:T(8,128)(2,1)S(1)} collective-permute-done((bf16[2048,256]{1,0:T(8,128)(2,1)S(1)}, bf16[2048,256]{1,0:T(8,128)(2,1)S(1)}, u32[]{:S(2)}, u32[]{:S(2)}) %collective-permute-start.4) | collective-permute-done | bytes 1048608 | tf_op jit(solution)/shard_map/ppermute | solution.py:19
  140.9 1.0 copy-done.5
  141.9 0.0 collective-permute-start.5
  141.9 23.7 %collective-permute-done.5 = bf16[2048,256]{1,0:T(8,128)(2,1)} collective-permute-done((bf16[2048,256]{1,0:T(8,128)(2,1)S(1)}, bf16[2048,256]{1,0:T(8,128)(2,1)}, u32[]{:S(2)}, u32[]{:S(2)}) %collective-permute-start.5) | collective-permute-done | bytes 1048608 | tf_op jit(solution)/shard_map/ppermute | solution.py:19
  165.6 0.0 collective-permute-start.6
  165.6 0.0 all-gather.2.cloned.1.call-update
  165.6 0.0 copy-start.6
  165.6 0.0 copy-start.4
  165.6 0.0 copy-start.2
  165.6 0.8 broadcast_multiply_fusion
  166.5 0.8 add.47
  167.3 29.8 %collective-permute-done.6 = bf16[2048,256]{1,0:T(8,128)(2,1)} collective-permute-done((bf16[2048,256]{1,0:T(8,128)(2,1)}, bf16[2048,256]{1,0:T(8,128)(2,1)}, u32[]{:S(2)}, u32[]{:S(2)}) %collective-permute-start.6) | collective-permute-done | bytes 1048608 | tf_op jit(solution)/shard_map/ppermute | solution.py:19
  197.1 1.4 constant_dynamic-update-slice_fusion.15
  198.4 1.6 constant_dynamic-update-slice_fusion.14
  200.0 1.4 constant_dynamic-update-slice_fusion.13
  201.4 1.4 constant_dynamic-update-slice_fusion.12
  202.8 1.4 constant_dynamic-update-slice_fusion.11
  204.1 0.1 constant_dynamic-update-slice_fusion.10
  204.3 0.1 constant_dynamic-update-slice_fusion.9
  204.4 1.4 constant_dynamic-update-slice_fusion.8
  205.8 1.4 constant_dynamic-update-slice_fusion.7
  207.2 1.4 constant_dynamic-update-slice_fusion.6
  208.6 0.0 copy-done.6
  208.6 0.1 constant_dynamic-update-slice_fusion.5
  208.7 0.1 constant_dynamic-update-slice_fusion.4
  208.9 0.0 copy-done.2
  208.9 0.1 constant_dynamic-update-slice_fusion.3
  209.0 0.1 constant_dynamic-update-slice_fusion.2
  209.2 0.1 constant_dynamic-update-slice_fusion.1
  209.3 0.1 constant_dynamic-update-slice_fusion
  209.5 3.6 %compare_select_fusion = f32[256,2048]{1,0:T(8,128)S(1)} fusion(bf16[2048,4096]{1,0:T(8,128)(2,1)S(1)} %constant_dynamic-update-slice_fusion, s32[]{:T(128)S(6)} %select_n.54, bf16[256,8192]{1,0:T(8,128)(2,1)} %param.6, s32[]{:T(128)S(6)} %select_n.52, s32[2048]{0:T(1024)S(1)} %add_select_fusion, s32[256]{0:T(256)S(1)} %add.47), kind=kOutput, calls=%fused_computation.3 | convolution fusion | flops 2148532224 | bytes 11543560 | tf_op jit(solution)/shard_map/dot_general | solution.py:35
  213.1 1.2 fusion.13
  214.4 12.2 %psum.7 = bf16[256,64]{1,0:T(8,128)(2,1)S(1)} all-reduce(f32[256,64]{1,0:T(8,128)S(1)} %fusion.13), channel_id=1, replica_groups=mesh['tp'=4,'ad'=8] {'tp'}, use_global_device_ids=true, to_apply=%region_0.1 | all-reduce | flops 16384 | bytes 98304 | tf_op jit(solution)/shard_map/psum | solution.py:44
  226.5 0.0 all-gather.2.cloned.1.call-done
  226.6 2.6 %fusion.8 = f32[256,512]{1,0:T(8,128)S(1)} fusion(bf16[2048,512]{1,0:T(8,128)(2,1)} %all-gather.2.cloned.1.call-done, s32[2048]{0:T(1024)S(1)} %add_select_fusion, s32[256]{0:T(256)S(1)} %add.47, s32[2048]{0:T(1024)S(1)} %fusion.19, bf16[256,64]{1,0:T(8,128)(2,1)S(1)} %psum.7), kind=kOutput, calls=%fused_computation.9 | convolution fusion | flops 605945856 | bytes 2671616 | tf_op jit(solution)/shard_map/dot_general | solution.py:54
  229.1 7.7 %fusion.6 = bf16[256,512]{1,0:T(8,128)(2,1)} fusion(f32[256,512]{1,0:T(8,128)S(1)} %fusion.8, bf16[256,8192]{1,0:T(8,128)(2,1)} %param.6, bf16[8192,512]{1,0:T(8,128)(2,1)} %param.7), kind=kOutput, calls=%fused_computation.7 | convolution fusion | flops 2147745792 | bytes 13369344 | tf_op jit(solution)/shard_map/dot_general | solution.py:27
  (8 shorter events, 0.0 us)
Async XLA Ops:
  6.5 202.8 %copy-start = (bf16[2048,256]{1,0:T(8,128)(2,1)S(1)}, bf16[2048,256]{1,0:T(8,128)(2,1)}, u32[]{:S(2)}) copy-start(bf16[2048,256]{1,0:T(8,128)(2,1)} %param.10) | copy-start | bytes 3145732
  6.5 220.0 %all-gather.2.cloned.1.call-start = ((), (), s32[]{:S(2)}) async-start(), calls=%async_computation | async-start | bytes 2359296 | tf_op jit(solution)/shard_map/all_gather | solution.py:45
  6.5 29.4 %collective-permute-start = (bf16[2048,256]{1,0:T(8,128)(2,1)}, bf16[2048,256]{1,0:T(8,128)(2,1)S(1)}, u32[]{:S(2)}, u32[]{:S(2)}) collective-permute-start(bf16[2048,256]{1,0:T(8,128)(2,1)} %param.10), channel_id=1, source_target_pairs={{0,1},{1,2},{2,3},{3,4},{4,5},{5,6},{6,7},{7,0},{8,9},{9,10},{10,1... | collective-permute-start | bytes 3145736 | tf_op jit(solution)/shard_map/ppermute | solution.py:19
  36.0 27.0 %collective-permute-start.1 = (bf16[2048,256]{1,0:T(8,128)(2,1)S(1)}, bf16[2048,256]{1,0:T(8,128)(2,1)S(1)}, u32[]{:S(2)}, u32[]{:S(2)}) collective-permute-start(bf16[2048,256]{1,0:T(8,128)(2,1)S(1)} %collective-permute-done), channel_id=1, source_target_pairs={{0,1},{1,2},{2,3},{3,4},{4,5},{5,6},{6,7},{7,0},{8,9},{9,10},{10,1... | collective-permute-start | bytes 3145736 | tf_op jit(solution)/shard_map/ppermute | solution.py:19
  63.0 26.2 %collective-permute-start.2 = (bf16[2048,256]{1,0:T(8,128)(2,1)S(1)}, bf16[2048,256]{1,0:T(8,128)(2,1)S(1)}, u32[]{:S(2)}, u32[]{:S(2)}) collective-permute-start(bf16[2048,256]{1,0:T(8,128)(2,1)S(1)} %collective-permute-done.1), channel_id=1, source_target_pairs={{0,1},{1,2},{2,3},{3,4},{4,5},{5,6},{6,7},{7,0},{8,9},{9,10},{10,1... | collective-permute-start | bytes 3145736 | tf_op jit(solution)/shard_map/ppermute | solution.py:19
  89.2 1.0 copy-start.1
  90.1 25.3 %collective-permute-start.3 = (bf16[2048,256]{1,0:T(8,128)(2,1)S(1)}, bf16[2048,256]{1,0:T(8,128)(2,1)S(1)}, u32[]{:S(2)}, u32[]{:S(2)}) collective-permute-start(bf16[2048,256]{1,0:T(8,128)(2,1)S(1)} %collective-permute-done.2), channel_id=1, source_target_pairs={{0,1},{1,2},{2,3},{3,4},{4,5},{5,6},{6,7},{7,0},{8,9},{9,10},{10,1... | collective-permute-start | bytes 3145736 | tf_op jit(solution)/shard_map/ppermute | solution.py:19
  115.4 1.0 copy-start.3
  116.4 24.5 %collective-permute-start.4 = (bf16[2048,256]{1,0:T(8,128)(2,1)S(1)}, bf16[2048,256]{1,0:T(8,128)(2,1)S(1)}, u32[]{:S(2)}, u32[]{:S(2)}) collective-permute-start(bf16[2048,256]{1,0:T(8,128)(2,1)S(1)} %collective-permute-done.3), channel_id=1, source_target_pairs={{0,1},{1,2},{2,3},{3,4},{4,5},{5,6},{6,7},{7,0},{8,9},{9,10},{10,1... | collective-permute-start | bytes 3145736 | tf_op jit(solution)/shard_map/ppermute | solution.py:19
  140.9 1.0 copy-start.5
  141.9 23.7 %collective-permute-start.5 = (bf16[2048,256]{1,0:T(8,128)(2,1)S(1)}, bf16[2048,256]{1,0:T(8,128)(2,1)}, u32[]{:S(2)}, u32[]{:S(2)}) collective-permute-start(bf16[2048,256]{1,0:T(8,128)(2,1)S(1)} %collective-permute-done.4), channel_id=1, source_target_pairs={{0,1},{1,2},{2,3},{3,4},{4,5},{5,6},{6,7},{7,0},{8,9},{9,10},{10,1... | collective-permute-start | bytes 3145736 | tf_op jit(solution)/shard_map/ppermute | solution.py:19
  165.6 31.5 %collective-permute-start.6 = (bf16[2048,256]{1,0:T(8,128)(2,1)}, bf16[2048,256]{1,0:T(8,128)(2,1)}, u32[]{:S(2)}, u32[]{:S(2)}) collective-permute-start(bf16[2048,256]{1,0:T(8,128)(2,1)} %collective-permute-done.5), channel_id=1, source_target_pairs={{0,1},{1,2},{2,3},{3,4},{4,5},{5,6},{6,7},{7,0},{8,9},{9,10},{10,1... | collective-permute-start | bytes 3145736 | tf_op jit(solution)/shard_map/ppermute | solution.py:19
  165.6 42.9 %copy-start.6 = (bf16[2048,256]{1,0:T(8,128)(2,1)S(1)}, bf16[2048,256]{1,0:T(8,128)(2,1)}, u32[]{:S(2)}) copy-start(bf16[2048,256]{1,0:T(8,128)(2,1)} %copy-done.5) | copy-start | bytes 3145732
  165.6 43.1 %copy-start.4 = (bf16[2048,256]{1,0:T(8,128)(2,1)S(1)}, bf16[2048,256]{1,0:T(8,128)(2,1)}, u32[]{:S(2)}) copy-start(bf16[2048,256]{1,0:T(8,128)(2,1)} %copy-done.3) | copy-start | bytes 3145732
  165.6 43.2 %copy-start.2 = (bf16[2048,256]{1,0:T(8,128)(2,1)S(1)}, bf16[2048,256]{1,0:T(8,128)(2,1)}, u32[]{:S(2)}) copy-start(bf16[2048,256]{1,0:T(8,128)(2,1)} %copy-done.1) | copy-start | bytes 3145732
Sparse Core Ops, SparseCore 0:
  165.7 55.8 all-gather.1
